TPU v7x, 32 devices: a whole 2x2x4 slice. The times are simulated.
32 devices in a mesh: row: 4 (over y, x), col: 8 (over z, core).
Axes of the slice: x: 2, y: 2, z: 4, core: 2. Of those that a mesh axis runs over, the one named last changes fastest.
Arguments:
- queries: float32 [2, 192, 20480], P(None, 'col', 'row'), may hold values from -6 to 6
- precond: float32 [20480, 20480], P('row', 'col'), may hold values from -0.0390625 to 0.0390625
- column_gain: float32 [20480], P('col'), may hold values from 0.5 to 2
- store: bfloat16 [12288, 20480], P('row', 'col'), may hold values from -0.0390625 to 0.0390625
Outputs:
- scores: float32 [2, 192, 12288], P(None, 'col', 'row')
All inputs are finite; a program needn't handle non-finite values.
Results may differ from a plain program's by a relative error of at most 0.0029.
Values sent between devices are 32-bit elements; how exact they have to be, the bound alone decides.
No kernel may reach another device: no remote copies, remote signals or barrier semaphores. Data moves between devices by JAX's collectives and lax.ppermute only.
A program may use at most 128 MiB of HBM per device.

v0:
```python
import jax
import jax.numpy as jnp
from jax import lax
from jax.sharding import PartitionSpec as P


def score_block(lowered, store):
    return lax.dot_general(
        lowered, store, (((1,), (1,)), ((), ())), preferred_element_type=jnp.float32
    )


def local(queries, precond, column_gain, store):
    results = []
    for batch_index in range(queries.shape[0]):
        local_rows = queries[batch_index]
        partial_rows = jnp.dot(
            lax.all_gather(local_rows, "col", axis=0, tiled=True),
            precond,
            precision=lax.Precision.HIGHEST,
            preferred_element_type=jnp.float32,
        )
        summed = lax.psum(partial_rows, "row")
        lowered = (summed * column_gain[None, :]).astype(jnp.bfloat16)
        own_scores = lax.psum_scatter(
            score_block(lowered, store), "col", scatter_dimension=0, tiled=True
        )
        results.append(own_scores)
    return jnp.stack(results)


def solution(mesh):
    return jax.shard_map(
        local,
        mesh=mesh,
        in_specs=(P(None, "col", "row"), P("row", "col"), P("col"), P("row", "col")),
        out_specs=P(None, "col", "row"),
        check_vma=False,
    )
```

profile of v0, /device:TPU:0, one launch (start us, length us, event | category | flops | bytes accessed | tf_op | source)
XLA Modules:
  0.0 335.7 jit_solution(14430148058530714590)
XLA Ops:
  6.5 0.0 all-gather.5.cloned.1.call-start
  6.5 2.2 fusion.8
  8.7 0.0 all-gather.5.cloned.1.call-update
  8.8 0.0 all-gather.7.cloned.1.call-start
  8.8 0.7 all-gather.7.cloned.1.call-update
  9.5 0.0 all-reduce.3.cloned.1.call-start
  9.6 46.9 %all-gather.5.cloned.1.call-done = f32[1,192,5120]{2,1,0:T(8,128)} async-done(((f32[1,24,5120]{2,1,0:T(8,128)}), f32[1,192,5120]{2,1,0:T(8,128)}) %all-gather.5.cloned.1.call-update) | async-done | bytes 3932176 | tf_op jit(solution)/shard_map/all_gather | solution.py:18
  56.4 38.3 %fusion.2 = f32[192,2560]{1,0:T(8,128)} fusion(f32[5120,2560]{1,0:T(8,128)} %param.5, f32[1,192,5120]{2,1,0:T(8,128)} %all-gather.5.cloned.1.call-done), kind=kOutput, calls=%fused_computation.2 | convolution fusion | flops 30198988800 | bytes 58327040 | tf_op jit(solution)/shard_map/dot_general | solution.py:17
  94.7 7.0 %all-gather.7.cloned.1.call-done = f32[1,192,5120]{2,1,0:T(8,128)} async-done(((f32[1,24,5120]{2,1,0:T(8,128)}), f32[1,192,5120]{2,1,0:T(8,128)}) %all-gather.7.cloned.1.call-update) | async-done | bytes 3932176 | tf_op jit(solution)/shard_map/all_gather | solution.py:18
  101.7 38.3 %fusion = f32[192,2560]{1,0:T(8,128)} fusion(f32[5120,2560]{1,0:T(8,128)} %param.5, f32[1,192,5120]{2,1,0:T(8,128)} %all-gather.7.cloned.1.call-done), kind=kOutput, calls=%fused_computation | convolution fusion | flops 30198988800 | bytes 58327040 | tf_op jit(solution)/shard_map/dot_general | solution.py:17
  140.0 0.0 copy-start.1
  140.0 0.0 all-reduce.3.cloned.1.call-update
  140.0 0.0 reduce-scatter.5.cloned.1.call-start
  140.1 99.0 %all-reduce.3.cloned.1.call-done = (f32[192,2560]{1,0:T(8,128)}, f32[192,2560]{1,0:T(8,128)}) async-done(((f32[192,2560]{1,0:T(8,128)}, f32[192,2560]{1,0:T(8,128)}), (f32[192,2560]{1,0:T(8,128)}, f32[192,2560]{1,0:T(8,128)})) %all-reduce.3.cloned.1.call-update) | async-done | bytes 3932176 | tf_op jit(solution)/shard_map/psum | solution.py:23
  239.0 0.0 copy-done.1
  239.0 0.0 copy-start
  239.0 12.8 %fusion.5 = f32[192,3072]{1,0:T(8,128)} fusion(bf16[3072,2560]{1,0:T(8,128)(2,1)} %param.7, f32[192,2560]{1,0:T(8,128)} %get-tuple-element.5, f32[2560]{0:T(1024)S(1)} %copy-done.1), kind=kOutput, calls=%fused_computation.7 | convolution fusion | flops 3020881920 | bytes 20064256 | tf_op jit(solution)/shard_map/dot_general | solution.py:8
  251.9 0.0 reduce-scatter.5.cloned.1.call-update
  251.9 0.2 reduce-scatter.3.cloned.1.call-start
  252.1 0.0 copy-done
  252.2 12.1 %fusion.4 = f32[192,3072]{1,0:T(8,128)} fusion(bf16[3072,2560]{1,0:T(8,128)(2,1)} %param.7, f32[192,2560]{1,0:T(8,128)S(1)} %copy-done, f32[2560]{0:T(1024)S(1)} %copy-done.1), kind=kOutput, calls=%fused_computation.6 | convolution fusion | flops 3020881920 | bytes 20064256 | tf_op jit(solution)/shard_map/dot_general | solution.py:8
  264.3 0.0 reduce-scatter.3.cloned.1.call-update
  264.3 24.8 %reduce-scatter.5.cloned.1.call-done = f32[24,3072]{1,0:T(8,128)} async-done(((f32[192,3072]{1,0:T(8,128)}), f32[24,3072]{1,0:T(8,128)}) %reduce-scatter.5.cloned.1.call-update) | async-done | bytes 294928 | tf_op jit(solution)/shard_map/reduce_scatter | solution.py:25
  289.1 38.2 %reduce-scatter.3.cloned.1.call-done = f32[24,3072]{1,0:T(8,128)} async-done(((f32[192,3072]{1,0:T(8,128)}), f32[24,3072]{1,0:T(8,128)}) %reduce-scatter.3.cloned.1.call-update) | async-done | bytes 294928 | tf_op jit(solution)/shard_map/reduce_scatter | solution.py:25
  327.3 1.9 pad_maximum_fusion
Async XLA Ops:
  6.5 49.9 %all-gather.5.cloned.1.call-start = ((), (), s32[]{:S(2)}) async-start(), calls=%async_computation.4 | async-start | bytes 4423680 | tf_op jit(solution)/shard_map/all_gather | solution.py:18
  8.8 92.9 %all-gather.7.cloned.1.call-start = ((), (), s32[]{:S(2)}) async-start(), calls=%async_computation.5 | async-start | bytes 4423680 | tf_op jit(solution)/shard_map/all_gather | solution.py:18
  9.5 229.5 %all-reduce.3.cloned.1.call-start = ((), (), s32[]{:S(2)}) async-start(), calls=%async_computation.6 | async-start | bytes 7864320 | tf_op jit(solution)/shard_map/psum | solution.py:23
  140.0 99.1 %copy-start.1 = (f32[2560]{0:T(1024)S(1)}, f32[2560]{0:T(1024)}, u32[]{:S(2)}) copy-start(f32[2560]{0:T(1024)} %param.6) | copy-start | bytes 30724
  140.0 149.1 %reduce-scatter.5.cloned.1.call-start = ((), (), s32[]{:S(2)}) async-start(), calls=%async_computation.3 | async-start | bytes 2654208 | tf_op jit(solution)/shard_map/reduce_scatter | solution.py:25
  239.0 13.1 %copy-start = (f32[192,2560]{1,0:T(8,128)S(1)}, f32[192,2560]{1,0:T(8,128)}, u32[]{:S(2)}) copy-start(f32[192,2560]{1,0:T(8,128)} %get-tuple-element.6) | copy-start | bytes 5898244
  251.9 75.4 %reduce-scatter.3.cloned.1.call-start = ((), (), s32[]{:S(2)}) async-start(), calls=%async_computation.2 | async-start | bytes 2654208 | tf_op jit(solution)/shard_map/reduce_scatter | solution.py:25
Sparse Core Ops, SparseCore 0:
  9.0 47.4 all-gather.4
  58.1 43.5 all-gather.6
  140.1 98.8 all-reduce.2
  252.0 37.0 reduce-scatter.4
  291.3 35.9 reduce-scatter.2
where the time goes:
time: 336 us
  waiting for transfers between devices  217 us (65%)
  matrix products  102 us (30%)
  between operations  13.2 us (4%)
    psum x1, waiting for transfers between devices, local(): summed = lax.psum(partial_rows, 'row')  99 us
    dot_general x2, matrix products, local(): jnp.dot(lax.all_gather(local_rows, 'col', axis=0, tiled=True), precond, p...  76.6 us
    reduce_scatter x2, waiting for transfers between devices, local(): lax.psum_scatter(score_block(lowered, store), 'col', scatter_dimension=0,...  63 us
    all_gather x2, waiting for transfers between devices, local(): lax.all_gather(local_rows, 'col', axis=0, tiled=True)  53.8 us
    dot_general x2, matrix products, score_block(): lax.dot_general(lowered, store, (((1,), (1,)), ((), ())), preferred_eleme...  25 us
  transfers between devices with their start and end apart: 5, of which 5 were waited for; matrix products, arithmetic and copies ran while one was open for 15% of the time, Pallas kernels for 0%

commit v1 on v0

--- a/solution.py
+++ b/solution.py
@@ -20,7 +20,7 @@
             precision=lax.Precision.HIGHEST,
             preferred_element_type=jnp.float32,
         )
-        summed = lax.psum(partial_rows, "row")
+        summed = jnp.sum(jax.lax.all_gather(partial_rows, "row"), 0)
         lowered = (summed * column_gain[None, :]).astype(jnp.bfloat16)
         own_scores = lax.psum_scatter(
             score_block(lowered, store), "col", scatter_dimension=0, tiled=True

time: 336 us -> 357 us (1.062)
  waiting for transfers between devices: 217 us -> 228 us
  other arithmetic: 1.9 us -> 10.2 us
    all_gather x0 -> x2, waiting for transfers between devices: none -> 113 us  [local(): summed = jnp.sum(jax.lax.all_gather(partial_rows, 'row'), 0)]
    psum x1 -> x0, waiting for transfers between devices: 99 us -> none  [local(): summed = lax.psum(partial_rows, 'row')]
    reduce_sum x0 -> x2, other arithmetic: none -> 8.34 us  [local(): summed = jnp.sum(jax.lax.all_gather(partial_rows, 'row'), 0)]
  transfers between devices with their start and end apart: 5 -> 6, of which waited for: 5 -> 6; matrix products, arithmetic and copies ran while one was open for 15% -> 31% of each run, Pallas kernels for 0% -> 0%
where the time goes in v1:
time: 357 us; the launch traced here: 356 us
  waiting for transfers between devices  228 us (64%)
  matrix products  102 us (29%)
  between operations  13.5 us (4%)
  other arithmetic  10.2 us (3%)
    all_gather x2, waiting for transfers between devices, local(): summed = jnp.sum(jax.lax.all_gather(partial_rows, 'row'), 0)  113 us
    dot_general x2, matrix products, local(): jnp.dot(lax.all_gather(local_rows, 'col', axis=0, tiled=True), precond, p...  76.7 us
    reduce_scatter x2, waiting for transfers between devices, local(): lax.psum_scatter(score_block(lowered, store), 'col', scatter_dimension=0,...  60.8 us
    all_gather x2, waiting for transfers between devices, local(): lax.all_gather(local_rows, 'col', axis=0, tiled=True)  53.8 us
    dot_general x2, matrix products, score_block(): lax.dot_general(lowered, store, (((1,), (1,)), ((), ())), preferred_eleme...  25.3 us
    reduce_sum x2, other arithmetic, local(): summed = jnp.sum(jax.lax.all_gather(partial_rows, 'row'), 0)  8.34 us
  transfers between devices with their start and end apart: 6, of which 6 were waited for; matrix products, arithmetic and copies ran while one was open for 31% of the time, Pallas kernels for 0%

profile of v1, /device:TPU:0, one launch (start us, length us, event | category | flops | bytes accessed | tf_op | source)
XLA Modules:
  0.0 356.4 jit_solution(12187104062120068040)
XLA Ops:
  6.5 0.0 all-gather.9.cloned.1.call-start
  6.5 2.2 fusion.8
  8.7 0.0 all-gather.9.cloned.1.call-update
  8.7 0.0 all-gather.13.cloned.1.call-start
  8.8 0.7 all-gather.13.cloned.1.call-update
  9.5 0.0 all-gather.11.cloned.1.call-start
  9.5 46.9 %all-gather.9.cloned.1.call-done = f32[1,192,5120]{2,1,0:T(8,128)} async-done(((f32[1,24,5120]{2,1,0:T(8,128)}), f32[1,192,5120]{2,1,0:T(8,128)}) %all-gather.9.cloned.1.call-update) | async-done | bytes 3932176 | tf_op jit(solution)/shard_map/all_gather | solution.py:18
  56.4 38.3 %fusion.2 = f32[192,2560]{1,0:T(8,128)} fusion(f32[5120,2560]{1,0:T(8,128)} %param.5, f32[1,192,5120]{2,1,0:T(8,128)} %all-gather.9.cloned.1.call-done), kind=kOutput, calls=%fused_computation.2 | convolution fusion | flops 30198988800 | bytes 58327040 | tf_op jit(solution)/shard_map/dot_general | solution.py:17
  94.7 0.0 all-gather.11.cloned.1.call-update
  94.8 0.0 all-gather.15.cloned.1.call-start
  94.8 6.9 %all-gather.13.cloned.1.call-done = f32[1,192,5120]{2,1,0:T(8,128)} async-done(((f32[1,24,5120]{2,1,0:T(8,128)}), f32[1,192,5120]{2,1,0:T(8,128)}) %all-gather.13.cloned.1.call-update) | async-done | bytes 3932176 | tf_op jit(solution)/shard_map/all_gather | solution.py:18
  101.7 38.4 %fusion = f32[192,2560]{1,0:T(8,128)} fusion(f32[5120,2560]{1,0:T(8,128)} %param.5, f32[1,192,5120]{2,1,0:T(8,128)} %all-gather.13.cloned.1.call-done), kind=kOutput, calls=%fused_computation | convolution fusion | flops 30198988800 | bytes 58327040 | tf_op jit(solution)/shard_map/dot_general | solution.py:17
  140.1 0.0 all-gather.15.cloned.1.call-update
  140.1 0.0 reduce-scatter.3.cloned.1.call-start
  140.1 45.4 %all-gather.11.cloned.1.call-done = f32[768,2560]{1,0:T(8,128)} async-done(((f32[192,2560]{1,0:T(8,128)}), f32[768,2560]{1,0:T(8,128)}) %all-gather.11.cloned.1.call-update) | async-done | bytes 7864336 | tf_op jit(solution)/shard_map/all_gather | solution.py:23
  185.5 0.0 copy-start
  185.5 4.2 %reduce_sum.18 = f32[192,2560]{1,0:T(8,128)S(1)} reduce(f32[4,192,2560]{2,1,0:T(8,128)} %bitcast.15, f32[]{:T(128)} %constant.0.clone.1), dimensions={0}, to_apply=%region_0.0 | reduce | flops 1474560 | bytes 9830404 | tf_op jit(solution)/shard_map/reduce_sum | solution.py:23
  189.7 0.0 copy-done
  189.7 13.0 %fusion.4 = f32[192,3072]{1,0:T(8,128)} fusion(bf16[3072,2560]{1,0:T(8,128)(2,1)} %param.7, f32[192,2560]{1,0:T(8,128)S(1)} %reduce_sum.18, f32[2560]{0:T(1024)S(1)} %copy-done), kind=kOutput, calls=%fused_computation.6 | convolution fusion | flops 3020881920 | bytes 20064256 | tf_op jit(solution)/shard_map/dot_general | solution.py:8
  202.7 0.0 reduce-scatter.3.cloned.1.call-update
  202.7 0.2 reduce-scatter.5.cloned.1.call-start
  202.9 67.4 %all-gather.15.cloned.1.call-done = f32[768,2560]{1,0:T(8,128)} async-done(((f32[192,2560]{1,0:T(8,128)}), f32[768,2560]{1,0:T(8,128)}) %all-gather.15.cloned.1.call-update) | async-done | bytes 7864336 | tf_op jit(solution)/shard_map/all_gather | solution.py:23
  270.3 4.2 %reduce_sum.19 = f32[192,2560]{1,0:T(8,128)S(1)} reduce(f32[4,192,2560]{2,1,0:T(8,128)} %bitcast.14, f32[]{:T(128)} %constant.0.clone.1), dimensions={0}, to_apply=%region_2.0 | reduce | flops 1474560 | bytes 9830404 | tf_op jit(solution)/shard_map/reduce_sum | solution.py:23
  274.5 12.3 %fusion.5 = f32[192,3072]{1,0:T(8,128)} fusion(bf16[3072,2560]{1,0:T(8,128)(2,1)} %param.7, f32[192,2560]{1,0:T(8,128)S(1)} %reduce_sum.19, f32[2560]{0:T(1024)S(1)} %copy-done), kind=kOutput, calls=%fused_computation.7 | convolution fusion | flops 3020881920 | bytes 20064256 | tf_op jit(solution)/shard_map/dot_general | solution.py:8
  286.9 0.0 reduce-scatter.5.cloned.1.call-update
  286.9 22.7 %reduce-scatter.3.cloned.1.call-done = f32[24,3072]{1,0:T(8,128)} async-done(((f32[192,3072]{1,0:T(8,128)}), f32[24,3072]{1,0:T(8,128)}) %reduce-scatter.3.cloned.1.call-update) | async-done | bytes 294928 | tf_op jit(solution)/shard_map/reduce_scatter | solution.py:25
  309.6 38.1 %reduce-scatter.5.cloned.1.call-done = f32[24,3072]{1,0:T(8,128)} async-done(((f32[192,3072]{1,0:T(8,128)}), f32[24,3072]{1,0:T(8,128)}) %reduce-scatter.5.cloned.1.call-update) | async-done | bytes 294928 | tf_op jit(solution)/shard_map/reduce_scatter | solution.py:25
  347.7 1.9 pad_maximum_fusion
Async XLA Ops:
  6.5 49.9 %all-gather.9.cloned.1.call-start = ((), (), s32[]{:S(2)}) async-start(), calls=%async_computation.4 | async-start | bytes 4423680 | tf_op jit(solution)/shard_map/all_gather | solution.py:18
  8.7 93.0 %all-gather.13.cloned.1.call-start = ((), (), s32[]{:S(2)}) async-start(), calls=%async_computation.6 | async-start | bytes 4423680 | tf_op jit(solution)/shard_map/all_gather | solution.py:18
  9.5 176.0 %all-gather.11.cloned.1.call-start = ((), (), s32[]{:S(2)}) async-start(), calls=%async_computation.5 | async-start | bytes 9830400 | tf_op jit(solution)/shard_map/all_gather | solution.py:23
  94.8 175.6 %all-gather.15.cloned.1.call-start = ((), (), s32[]{:S(2)}) async-start(), calls=%async_computation.7 | async-start | bytes 9830400 | tf_op jit(solution)/shard_map/all_gather | solution.py:23
  140.1 169.5 %reduce-scatter.3.cloned.1.call-start = ((), (), s32[]{:S(2)}) async-start(), calls=%async_computation.2 | async-start | bytes 2654208 | tf_op jit(solution)/shard_map/reduce_scatter | solution.py:25
  185.5 4.2 %copy-start = (f32[2560]{0:T(1024)S(1)}, f32[2560]{0:T(1024)}, u32[]{:S(2)}) copy-start(f32[2560]{0:T(1024)} %param.6) | copy-start | bytes 30724
  202.7 145.0 %reduce-scatter.5.cloned.1.call-start = ((), (), s32[]{:S(2)}) async-start(), calls=%async_computation.3 | async-start | bytes 2654208 | tf_op jit(solution)/shard_map/reduce_scatter | solution.py:25
Sparse Core Ops, SparseCore 0:
  9.0 47.4 all-gather.8
  58.1 43.5 all-gather.12
  103.5 81.8 all-gather.10
  187.2 83.1 all-gather.14
  272.5 37.0 reduce-scatter.2
  311.8 35.8 reduce-scatter.4
